TPU v7x, 256 devices: a whole 4x4x8 slice. The times are simulated.
256 devices in a mesh: row: 16 (over x_lo, y, core), col: 16 (over z, x_hi).
Axes of the slice: x: 4 (x_hi: 2, x_lo: 2; x = x_hi * 2 + x_lo), y: 4, z: 8, core: 2. Of those that a mesh axis runs over, the one named last changes fastest.
Arguments:
- block_vecs: float32 [16, 131072], P(None, ('col', 'row')), may hold values from -130 to 130
- direction: float32 [16, 131072], P(None, ('col', 'row')), may hold values from -130 to 130
- blocks: bfloat16 [1024, 32, 128, 128], P('col', 'row'), may hold values from 0 to 4
- block_cols: int32 [1024, 32], P('col', 'row'), may hold values from 0 to 1023, as said below
- live_counts: int32 [1024, 16], P('col', 'row'), may hold values from 1 to 2, as said below
Outputs:
- x_next: float32 [16, 131072], P(None, ('col', 'row'))
- reduced: float32 [48, 48], replicated
- residual: float32 [16, 131072], P(None, ('col', 'row'))
Inputs may be any that keep to these rules, and one draw needn't show every extreme that they name: `block_cols`: A block column index g in slots 2 * r to 2 * r + 1 of any block row satisfies (g // 4) mod 16 == r. `live_counts`: every block row has 2 live slots in at least one segment.
All inputs are finite; a program needn't handle non-finite values.
Results may differ from a plain program's by a relative error of at most 0.0003.
Values sent between devices are 32-bit elements; how exact they have to be, the bound alone decides.
A program may use at most 64 MiB of HBM per device.

v0:
```python
import math
import jax
import jax.numpy as jnp
from jax import lax
from jax.sharding import PartitionSpec as P

highest = lax.Precision.HIGHEST


def outer(left, right):
    return jnp.dot(left, right.T, precision=highest, preferred_element_type=jnp.float32)


def cholesky_lower(matrix):
    order_small = matrix.shape[0]
    places = jnp.arange(order_small, dtype=jnp.int32)

    def column_step(step, lower):
        pick = (places == step).astype(jnp.float32)
        row_now = jnp.sum(lower * pick[:, None], axis=0)
        column_now = jnp.sum(matrix * pick[None, :], axis=1)
        pivot = jnp.sum(column_now * pick) - jnp.sum(row_now * row_now)
        pivot_root = jnp.sqrt(pivot)
        below = (column_now - jnp.sum(lower * row_now[None, :], axis=1)) / pivot_root
        values = jnp.where(places > step, below, jnp.where(places == step, pivot_root, 0.0))
        return lower + values[:, None] * pick[None, :]

    return lax.fori_loop(0, order_small, column_step, jnp.zeros_like(matrix))


def solve_lower(lower, right):
    order_small = lower.shape[0]
    places = jnp.arange(order_small, dtype=jnp.int32)

    def row_step(step, solved):
        pick = (places == step).astype(jnp.float32)
        row_now = jnp.sum(lower * pick[:, None], axis=0)
        pivot = jnp.sum(row_now * pick)
        right_row = jnp.sum(right * pick[:, None], axis=0)
        value = (right_row - jnp.sum(row_now[:, None] * solved, axis=0)) / pivot
        return solved + pick[:, None] * value[None, :]

    return lax.fori_loop(0, order_small, row_step, jnp.zeros_like(right))


def solve_upper_t(lower, right):
    order_small = lower.shape[0]
    places = jnp.arange(order_small, dtype=jnp.int32)

    def row_step(count, solved):
        step = order_small - 1 - count
        pick = (places == step).astype(jnp.float32)
        column_now = jnp.sum(lower * pick[None, :], axis=1)
        pivot = jnp.sum(column_now * pick)
        right_row = jnp.sum(right * pick[:, None], axis=0)
        value = (right_row - jnp.sum(column_now[:, None] * solved, axis=0)) / pivot
        return solved + pick[:, None] * value[None, :]

    return lax.fori_loop(0, order_small, row_step, jnp.zeros_like(right))


def local_layout(block_cols, live_counts, span_rows, block_size, row_count):
    per_span = span_rows // block_size
    span_index = block_cols // per_span
    local_cols = span_index // row_count * per_span + block_cols % per_span
    slot_count = block_cols.shape[1]
    live_mask = (jnp.arange(slot_count, dtype=jnp.int32)[None, :] < live_counts).astype(jnp.float32)
    return (local_cols, live_mask)


def forward_part(col_panel, blocks, local_cols, live_mask):
    vec_width = col_panel.shape[0]
    block_size = blocks.shape[2]
    col_blocks = col_panel.reshape(vec_width, -1, block_size)
    picked = col_blocks[:, local_cols, :] * live_mask[None, :, :, None]
    forward = jnp.einsum(
        "vbkj,bkij->vbi", picked, blocks, precision=highest, preferred_element_type=jnp.float32
    )
    return 0.5 * forward.reshape(vec_width, -1)


def backward_part(row_panel, col_length, blocks, local_cols, live_mask):
    vec_width = row_panel.shape[0]
    block_size = blocks.shape[2]
    row_blocks = row_panel.reshape(vec_width, -1, block_size)
    backward = (
        jnp.einsum(
            "vbi,bkij->vbkj",
            row_blocks,
            blocks,
            precision=highest,
            preferred_element_type=jnp.float32,
        )
        * live_mask[None, :, :, None]
    )
    spread = jnp.zeros((vec_width, col_length // block_size, block_size), jnp.float32)
    spread = spread.at[:, local_cols.reshape(-1), :].add(
        backward.reshape(vec_width, -1, block_size)
    )
    return 0.5 * spread.reshape(vec_width, -1)


def per_device(block_vecs, direction, blocks, block_cols, live_counts):
    row_count = lax.axis_size("row")
    col_count = lax.axis_size("col")
    vec_width = block_vecs.shape[0]
    span_rows = block_vecs.shape[1]
    order_total = span_rows * row_count * col_count
    col_length = span_rows * col_count
    block_size = blocks.shape[2]
    local_cols, live_mask = local_layout(block_cols, live_counts, span_rows, block_size, row_count)
    paired = jnp.concatenate([block_vecs, direction], axis=0)
    pair_cols = lax.all_gather(paired, "col", axis=1, tiled=True)
    pair_rows = lax.all_gather(paired, "row", axis=1, tiled=True)
    forward = forward_part(pair_cols, blocks, local_cols, live_mask)
    backward = backward_part(pair_rows, col_length, blocks, local_cols, live_mask)
    image_pair = lax.psum_scatter(
        forward, "row", scatter_dimension=1, tiled=True
    ) + lax.psum_scatter(backward, "col", scatter_dimension=1, tiled=True)
    image_x = image_pair[:vec_width]
    image_p = image_pair[vec_width:]
    gram_x, cross_x = lax.psum(
        (outer(block_vecs, block_vecs), outer(block_vecs, image_x)), ("row", "col")
    )
    factor_x = cholesky_lower(gram_x)
    coefficient = solve_upper_t(factor_x, solve_lower(factor_x, cross_x))
    resid = image_x - jnp.dot(
        coefficient.T, block_vecs, precision=highest, preferred_element_type=jnp.float32
    )
    basis = jnp.concatenate([block_vecs, resid, direction], axis=0)
    resid_cols = lax.all_gather(resid, "col", axis=1, tiled=True)
    resid_rows = lax.all_gather(resid, "row", axis=1, tiled=True)
    forward_r = forward_part(resid_cols, blocks, local_cols, live_mask)
    column_x = outer(basis, image_x)
    column_p = outer(basis, image_p)
    backward_r = backward_part(resid_rows, col_length, blocks, local_cols, live_mask)
    image_r = lax.psum_scatter(
        forward_r, "row", scatter_dimension=1, tiled=True
    ) + lax.psum_scatter(backward_r, "col", scatter_dimension=1, tiled=True)
    column_r = outer(basis, image_r)
    gram_apply = jnp.concatenate([column_x, column_r, column_p], axis=1)
    gram_basis, gram_apply = lax.psum((outer(basis, basis), gram_apply), ("row", "col"))
    factor = cholesky_lower(gram_basis)
    halfway = solve_lower(factor, 0.5 * (gram_apply + gram_apply.T))
    reduced = solve_lower(factor, halfway.T)
    shifted = reduced + 3.0 * jnp.eye(3 * vec_width, dtype=jnp.float32)
    target = jnp.dot(
        shifted, shifted[:, :vec_width], precision=highest, preferred_element_type=jnp.float32
    )
    mixing = solve_upper_t(factor, target)
    fresh = jnp.dot(mixing.T, basis, precision=highest, preferred_element_type=jnp.float32)
    gram_fresh = lax.psum(outer(fresh, fresh), ("row", "col"))
    factor_fresh = cholesky_lower(gram_fresh)
    x_next = math.sqrt(order_total) * solve_lower(factor_fresh, fresh)
    return (x_next, reduced, resid)


def solution(mesh):
    return jax.shard_map(
        per_device,
        mesh=mesh,
        in_specs=(
            P(None, ("col", "row")),
            P(None, ("col", "row")),
            P("col", "row", None, None),
            P("col", "row"),
            P("col", "row"),
        ),
        out_specs=(P(None, ("col", "row")), P(), P(None, ("col", "row"))),
        check_vma=False,
    )
```

profile of v0, /device:TPU:1, one launch (start us, length us, event | category | flops | bytes accessed | tf_op | source)
XLA Modules:
  0.0 1421.3 jit_solution(11187509048310806808)
XLA Ops:
  11.9 37.2 %all-gather.5.cloned.1.call-done = f32[32,8192]{1,0:T(8,128)} async-done(((f32[32,512]{1,0:T(8,128)}), f32[32,8192]{1,0:T(8,128)}) %all-gather.5.cloned.1.call-update) | async-done | bytes 1048592 | tf_op jit(solution)/shard_map/all_gather | solution.py:114
  49.0 1.4 copy.57
  50.4 4.3 convolution_multiply_fusion
  54.9 5.7 scatter_fusion
  60.6 1.1 copy_bitcast_fusion
  62.0 64.4 %all-gather.3.cloned.1.call-done = f32[32,8192]{1,0:T(8,128)} async-done(((f32[32,512]{1,0:T(8,128)}), f32[32,8192]{1,0:T(8,128)}) %all-gather.3.cloned.1.call-update) | async-done | bytes 1048592 | tf_op jit(solution)/shard_map/all_gather | solution.py:113
  126.4 1.4 copy_bitcast_fusion.2
  128.6 6.0 fusion.45
  134.6 1.1 copy.69
  135.9 192.4 %reduce-scatter.7.cloned.1.call-done = f32[32,512]{1,0:T(8,128)} async-done(((f32[32,8192]{1,0:T(8,128)}), f32[32,512]{1,0:T(8,128)}) %reduce-scatter.7.cloned.1.call-update) | async-done | bytes 65552 | tf_op jit(solution)/shard_map/reduce_scatter | solution.py:119
  328.3 66.4 %reduce-scatter.5.cloned.1.call-done = f32[32,512]{1,0:T(8,128)} async-done(((f32[32,8192]{1,0:T(8,128)}), f32[32,512]{1,0:T(8,128)}) %reduce-scatter.5.cloned.1.call-update) | async-done | bytes 65552 | tf_op jit(solution)/shard_map/reduce_scatter | solution.py:117
  394.7 0.9 add.271
  395.7 78.8 %all-reduce.1 = (f32[16,16]{0,1:T(8,128)S(1)}, f32[16,16]{1,0:T(8,128)S(1)}) all-reduce(f32[16,16]{0,1:T(8,128)S(1)} %convolution_bitcast_fusion.1, f32[16,16]{1,0:T(8,128)S(1)} %fusion.72), channel_id=1, replica_groups=mesh['row'=16,'col'=16] {'row','col'}, use_global_device_ids=true, to_apply=%region_11.12 | all-reduce | flops 512 | bytes 4096 | tf_op jit(solution)/shard_map/psum | solution.py:122
  474.5 37.0 %while.135 = (s32[]{:T(128)}, f32[16,16]{1,0:T(8,128)S(1)}, f32[16,16]{1,0:T(8,128)S(1)}, s32[]{:T(128)}, s32[]{:T(128)}) while((s32[]{:T(128)}, f32[16,16]{1,0:T(8,128)S(1)}, f32[16,16]{1,0:T(8,128)S(1)}, s32[]{:T(128)}, s32[]{:T(128)}) %tuple.302), condition=%wide.region_10.11_spmd.clone.clone, body=%wide.region_4.10_spmd.clone.clone.sunk | while | flops 2978 | bytes 6069 | solution.py:28
  511.6 24.3 %while.129 = (s32[]{:T(128)}, f32[16,16]{1,0:T(8,128)S(1)}, f32[16,16]{1,0:T(8,128)S(1)}, f32[16,16]{1,0:T(8,128)S(1)}, s32[]{:T(128)}, /*index=5*/s32[]{:T(128)}) while((s32[]{:T(128)}, f32[16,16]{1,0:T(8,128)S(1)}, f32[16,16]{1,0:T(8,128)S(1)}, f32[16,16]{1,0:T(8,128)S(1)}, s32[]{:T(128)}, /*index=5*/s32[]{:T(128)}) %tuple.305), condition=%wide.region_17.18_spmd.clone, body=%wide.region_12.17_spmd.clone.sunk | while | flops 2626 | bytes 5984 | solution.py:43
  535.9 24.8 %while.130 = (s32[]{:T(128)}, f32[16,16]{1,0:T(8,128)S(1)}, f32[16,16]{1,0:T(8,128)S(1)}, f32[16,16]{1,0:T(8,128)S(1)}, s32[]{:T(128)}, /*index=5*/s32[]{:T(128)}, s32[]{:T(128)}) while((s32[]{:T(128)}, f32[16,16]{1,0:T(8,128)S(1)}, f32[16,16]{1,0:T(8,128)S(1)}, f32[16,16]{1,0:T(8,128)S(1)}, s32[]{:T(128)}, ...), condition=%wide.region_23.24_spmd.clone, body=%wide.region_18.23_spmd.clone.sunk | while | flops 2627 | bytes 6004 | solution.py:59
  560.9 19.6 %all_gather.15 = f32[16,8192]{1,0:T(8,128)S(1)} all-gather(f32[16,512]{1,0:T(8,128)S(1)} %convolution_subtract_fusion), channel_id=1, replica_groups=mesh['row'=16,'col'=16] {'row'}, dimensions={1}, use_global_device_ids=true | all-gather | bytes 557056 | tf_op jit(solution)/shard_map/all_gather | solution.py:132
  580.6 3.8 convolution_multiply_fusion.1
  584.5 5.2 scatter_fusion.1
  590.6 34.6 %all_gather.14 = f32[16,8192]{1,0:T(8,128)S(1)} all-gather(f32[16,512]{1,0:T(8,128)S(1)} %convolution_subtract_fusion), channel_id=1, replica_groups=mesh['row'=16,'col'=16] {'col'}, dimensions={1}, use_global_device_ids=true | all-gather | bytes 557056 | tf_op jit(solution)/shard_map/all_gather | solution.py:131
  626.0 5.2 fusion.49
  632.8 145.4 %reduce-scatter.11.cloned.1.call-done = f32[16,512]{1,0:T(8,128)} async-done(((f32[16,8192]{1,0:T(8,128)}), f32[16,512]{1,0:T(8,128)}) %reduce-scatter.11.cloned.1.call-update) | async-done | bytes 32784 | tf_op jit(solution)/shard_map/reduce_scatter | solution.py:139
  778.1 65.7 %reduce-scatter.9.cloned.1.call-done = f32[16,512]{1,0:T(8,128)} async-done(((f32[16,8192]{1,0:T(8,128)}), f32[16,512]{1,0:T(8,128)}) %reduce-scatter.9.cloned.1.call-update) | async-done | bytes 32784 | tf_op jit(solution)/shard_map/reduce_scatter | solution.py:137
  843.8 0.9 fusion.58
  844.8 79.4 %all-reduce = (f32[48,48]{0,1:T(8,128)S(1)}, f32[48,48]{1,0:T(8,128)S(1)}) all-reduce(f32[48,48]{0,1:T(8,128)S(1)} %pad_maximum_fusion.1, f32[48,48]{1,0:T(8,128)S(1)} %fusion.70), channel_id=1, replica_groups=mesh['row'=16,'col'=16] {'row','col'}, use_global_device_ids=true, to_apply=%region_35.36 | all-reduce | flops 4608 | bytes 36864 | tf_op jit(solution)/shard_map/psum | solution.py:142
  924.3 111.3 %while.136 = (s32[]{:T(128)}, f32[48,48]{1,0:T(8,128)S(1)}, f32[48,48]{1,0:T(8,128)S(1)}, s32[]{:T(128)}, s32[]{:T(128)}) while((s32[]{:T(128)}, f32[48,48]{1,0:T(8,128)S(1)}, f32[48,48]{1,0:T(8,128)S(1)}, s32[]{:T(128)}, s32[]{:T(128)}) %tuple.311), condition=%wide.region_31.32_spmd.clone.clone, body=%wide.region_25.31_spmd.clone.clone.sunk | while | flops 25826 | bytes 48693 | solution.py:28
  1035.6 79.4 %while.131 = (s32[]{:T(128)}, f32[48,48]{1,0:T(8,128)S(1)}, f32[48,48]{1,0:T(8,128)S(1)}, f32[48,48]{1,0:T(8,128)S(1)}, s32[]{:T(128)}, /*index=5*/s32[]{:T(128)}) while((s32[]{:T(128)}, f32[48,48]{1,0:T(8,128)S(1)}, f32[48,48]{1,0:T(8,128)S(1)}, f32[48,48]{1,0:T(8,128)S(1)}, s32[]{:T(128)}, /*index=5*/s32[]{:T(128)}) %tuple.314), condition=%wide.region_41.42_spmd.clone, body=%wide.region_36.41_spmd.clone.sunk | while | flops 23234 | bytes 48480 | solution.py:43
  1115.1 79.4 %while.132 = (s32[]{:T(128)}, f32[48,48]{1,0:T(8,128)S(1)}, f32[48,48]{1,0:T(8,128)S(1)}, f32[48,48]{1,0:T(8,128)S(1)}, s32[]{:T(128)}, /*index=5*/s32[]{:T(128)}) while((s32[]{:T(128)}, f32[48,48]{1,0:T(8,128)S(1)}, f32[48,48]{1,0:T(8,128)S(1)}, f32[48,48]{1,0:T(8,128)S(1)}, s32[]{:T(128)}, /*index=5*/s32[]{:T(128)}) %tuple.344), condition=%wide.region_47.48_spmd.clone, body=%wide.region_42.47_spmd.clone.sunk | while | flops 23234 | bytes 48480 | solution.py:43
  1194.8 81.8 %while.133 = (s32[]{:T(128)}, f32[48,16]{0,1:T(8,128)S(1)}, f32[48,16]{0,1:T(8,128)S(1)}, f32[48,48]{1,0:T(8,128)S(1)}, s32[]{:T(128)}, /*index=5*/s32[]{:T(128)}, s32[]{:T(128)}) while((s32[]{:T(128)}, f32[48,16]{0,1:T(8,128)S(1)}, f32[48,16]{0,1:T(8,128)S(1)}, f32[48,48]{1,0:T(8,128)S(1)}, s32[]{:T(128)}, ...), condition=%wide.region_53.54_spmd.clone, body=%wide.region_48.53_spmd.clone.sunk | while | flops 10947 | bytes 23348 | solution.py:59
  1276.8 73.6 %psum.39 = f32[16,16]{1,0:T(8,128)S(1)} all-reduce(f32[16,16]{1,0:T(8,128)S(1)} %fusion.73), channel_id=1, replica_groups=mesh['row'=16,'col'=16] {'row','col'}, use_global_device_ids=true, to_apply=%region_54.55 | all-reduce | flops 256 | bytes 2048 | tf_op jit(solution)/shard_map/psum | solution.py:152
  1350.5 37.0 %while.137 = (s32[]{:T(128)}, f32[16,16]{1,0:T(8,128)S(1)}, f32[16,16]{1,0:T(8,128)S(1)}, s32[]{:T(128)}, s32[]{:T(128)}) while((s32[]{:T(128)}, f32[16,16]{1,0:T(8,128)S(1)}, f32[16,16]{1,0:T(8,128)S(1)}, s32[]{:T(128)}, s32[]{:T(128)}) %tuple.323), condition=%wide.region_61.62_spmd.clone.clone, body=%wide.region_55.61_spmd.clone.clone.sunk | while | flops 2978 | bytes 6069 | solution.py:28
  1387.5 26.3 %while.134 = (s32[]{:T(128)}, f32[16,512]{1,0:T(8,128)S(1)}, f32[16,512]{1,0:T(8,128)S(1)}, f32[16,16]{1,0:T(8,128)S(1)}, s32[]{:T(128)}, /*index=5*/s32[]{:T(128)}) while((s32[]{:T(128)}, f32[16,512]{1,0:T(8,128)S(1)}, f32[16,512]{1,0:T(8,128)S(1)}, f32[16,16]{1,0:T(8,128)S(1)}, s32[]{:T(128)}, /*index=5*/s32[]{:T(128)}) %tuple.326), condition=%wide.region_67.68_spmd.clone, body=%wide.region_62.67_spmd.clone.sunk | while | flops 66114 | bytes 144928 | solution.py:43
  (1698 shorter events, 405.3 us)
Async XLA Ops:
  7.2 41.9 %all-gather.5.cloned.1.call-start = ((), (), s32[]{:S(2)}) async-start(), calls=%async_computation.6 | async-start | bytes 1114112 | tf_op jit(solution)/shard_map/all_gather | solution.py:114
  8.7 0.6 copy-start.4
  9.4 117.1 %all-gather.3.cloned.1.call-start = ((), (), s32[]{:S(2)}) async-start(), calls=%async_computation.4 | async-start | bytes 1114112 | tf_op jit(solution)/shard_map/all_gather | solution.py:113
  10.1 318.2 %reduce-scatter.7.cloned.1.call-start = ((), (), s32[]{:S(2)}) async-start(), calls=%async_computation.7 | async-start | bytes 1114112 | tf_op jit(solution)/shard_map/reduce_scatter | solution.py:119
  61.7 333.0 %reduce-scatter.5.cloned.1.call-start = ((), (), s32[]{:S(2)}) async-start(), calls=%async_computation.5 | async-start | bytes 1114112 | tf_op jit(solution)/shard_map/reduce_scatter | solution.py:117
  134.6 1.2 copy-start.1
  135.7 642.4 %reduce-scatter.11.cloned.1.call-start = ((), (), s32[]{:S(2)}) async-start(), calls=%async_computation.9 | async-start | bytes 557056 | tf_op jit(solution)/shard_map/reduce_scatter | solution.py:139
  560.9 715.6 %copy-start.2 = (f32[16,512]{1,0:T(8,128)}, f32[16,512]{1,0:T(8,128)S(1)}, u32[]{:S(2)}) copy-start(f32[16,512]{1,0:T(8,128)S(1)} %convolution_subtract_fusion) | copy-start | bytes 98308
  590.5 253.3 %reduce-scatter.9.cloned.1.call-start = ((), (), s32[]{:S(2)}) async-start(), calls=%async_computation.8 | async-start | bytes 557056 | tf_op jit(solution)/shard_map/reduce_scatter | solution.py:137
  626.0 6.1 copy-start.3
  1194.5 219.9 %copy-start = (f32[48,48]{1,0:T(8,128)}, f32[48,48]{1,0:T(8,128)S(1)}, u32[]{:S(2)}) copy-start(f32[48,48]{1,0:T(8,128)S(1)} %get-tuple-element.811) | copy-start | bytes 27652
Sparse Core Ops, SparseCore 0:
  9.8 39.1 all-gather.4
  51.6 74.7 all-gather.2
  130.3 198.0 reduce-scatter.6
  330.7 63.9 reduce-scatter.4
  590.6 187.4 reduce-scatter.10
  780.5 63.2 reduce-scatter.8
where the time goes:
time: 1430 us; the launch traced here: 1420 us
  waiting for transfers between devices  572 us (40%)
  other arithmetic  410 us (29%)
  blocking collectives  286 us (20%)
  loops' own time  107 us (7%)
  matrix products  21.8 us (2%)
  between operations  14.4 us (1%)
    reduce_scatter x1, waiting for transfers between devices, per_device(): lax.psum_scatter(backward, 'col', scatter_dimension=1, tiled=True)  192 us
    reduce_scatter x1, waiting for transfers between devices, per_device(): lax.psum_scatter(backward_r, 'col', scatter_dimension=1, tiled=True)  145 us
    another operation x3, loops' own time, cholesky_lower(): return lax.fori_loop(0, order_small, column_step, jnp.zeros_like(matrix))  105 us
    div x128, other arithmetic, row_step(): value = (right_row - jnp.sum(row_now[:, None] * solved, axis=0)) / pivot  87.9 us
    reduce_sum x128, other arithmetic, row_step(): pivot = jnp.sum(row_now * pick)  85.7 us
    psum x1, blocking collectives, per_device(): lax.psum((outer(basis, basis), gram_apply), ('row', 'col'))  79.4 us
    psum x1, blocking collectives, per_device(): lax.psum((outer(block_vecs, block_vecs), outer(block_vecs, image_x)), ('r...  78.8 us
    psum x1, blocking collectives, per_device(): gram_fresh = lax.psum(outer(fresh, fresh), ('row', 'col'))  73.6 us
  transfers between devices with their start and end apart: 6, of which 6 were waited for; matrix products, arithmetic and copies ran while one was open for 2% of the time, Pallas kernels for 0%

commit v1 on v0

--- a/solution.py
+++ b/solution.py
@@ -128,7 +128,9 @@
         coefficient.T, block_vecs, precision=highest, preferred_element_type=jnp.float32
     )
     basis = jnp.concatenate([block_vecs, resid, direction], axis=0)
-    resid_cols = lax.all_gather(resid, "col", axis=1, tiled=True)
+    resid_cols = jnp.concatenate(
+        lax.all_to_all(jnp.stack([resid] * lax.axis_size("col")), "col", 0, 0), axis=1
+    )
     resid_rows = lax.all_gather(resid, "row", axis=1, tiled=True)
     forward_r = forward_part(resid_cols, blocks, local_cols, live_mask)
     column_x = outer(basis, image_x)

time: 1430 us -> 1440 us (level)
  waiting for transfers between devices: 572 us -> 610 us
  blocking collectives: 286 us -> 251 us
    all_gather x1 -> x0, blocking collectives: 34.6 us -> none  [per_device(): resid_cols = lax.all_gather(resid, 'col', axis=1, tiled=True)]
    reduce_scatter x1, waiting for transfers between devices: 145 us -> 175 us  [per_device(): lax.psum_scatter(backward_r, 'col', scatter_dimension=1, tiled=True)]
  transfers between devices with their start and end apart: 6 -> 7, of which waited for: 6 -> 7; matrix products, arithmetic and copies ran while one was open for 2% -> 3% of each run, Pallas kernels for 0% -> 0%
where the time goes in v1:
time: 1440 us; the launch traced here: 1430 us
  waiting for transfers between devices  610 us (42%)
  other arithmetic  410 us (28%)
  blocking collectives  251 us (17%)
  loops' own time  107 us (7%)
  matrix products  21.8 us (2%)
  between operations  14.4 us (1%)
    reduce_scatter x1, waiting for transfers between devices, per_device(): lax.psum_scatter(backward, 'col', scatter_dimension=1, tiled=True)  192 us
    reduce_scatter x1, waiting for transfers between devices, per_device(): lax.psum_scatter(backward_r, 'col', scatter_dimension=1, tiled=True)  175 us
    another operation x3, loops' own time, cholesky_lower(): return lax.fori_loop(0, order_small, column_step, jnp.zeros_like(matrix))  105 us
    div x128, other arithmetic, row_step(): value = (right_row - jnp.sum(row_now[:, None] * solved, axis=0)) / pivot  87.9 us
    reduce_sum x128, other arithmetic, row_step(): pivot = jnp.sum(row_now * pick)  85.7 us
    psum x1, blocking collectives, per_device(): lax.psum((outer(basis, basis), gram_apply), ('row', 'col'))  79.4 us
    psum x1, blocking collectives, per_device(): lax.psum((outer(block_vecs, block_vecs), outer(block_vecs, image_x)), ('r...  78.8 us
    psum x1, blocking collectives, per_device(): gram_fresh = lax.psum(outer(fresh, fresh), ('row', 'col'))  73.6 us
  transfers between devices with their start and end apart: 7, of which 7 were waited for; matrix products, arithmetic and copies ran while one was open for 3% of the time, Pallas kernels for 0%

profile of v1, /device:TPU:1, one launch (start us, length us, event | category | flops | bytes accessed | tf_op | source)
XLA Modules:
  0.0 1431.8 jit_solution(15068431874640594212)
XLA Ops:
  11.9 37.2 %all-gather.5.cloned.1.call-done = f32[32,8192]{1,0:T(8,128)} async-done(((f32[32,512]{1,0:T(8,128)}), f32[32,8192]{1,0:T(8,128)}) %all-gather.5.cloned.1.call-update) | async-done | bytes 1048592 | tf_op jit(solution)/shard_map/all_gather | solution.py:114
  49.0 1.4 copy.70
  50.4 4.3 convolution_multiply_fusion
  54.9 5.7 scatter_fusion
  60.6 1.1 copy_bitcast_fusion
  62.0 64.4 %all-gather.3.cloned.1.call-done = f32[32,8192]{1,0:T(8,128)} async-done(((f32[32,512]{1,0:T(8,128)}), f32[32,8192]{1,0:T(8,128)}) %all-gather.3.cloned.1.call-update) | async-done | bytes 1048592 | tf_op jit(solution)/shard_map/all_gather | solution.py:113
  126.4 1.4 copy_bitcast_fusion.2
  128.6 6.0 fusion.45
  134.6 1.1 copy.81
  135.9 192.4 %reduce-scatter.7.cloned.1.call-done = f32[32,512]{1,0:T(8,128)} async-done(((f32[32,8192]{1,0:T(8,128)}), f32[32,512]{1,0:T(8,128)}) %reduce-scatter.7.cloned.1.call-update) | async-done | bytes 65552 | tf_op jit(solution)/shard_map/reduce_scatter | solution.py:119
  328.3 66.4 %reduce-scatter.5.cloned.1.call-done = f32[32,512]{1,0:T(8,128)} async-done(((f32[32,8192]{1,0:T(8,128)}), f32[32,512]{1,0:T(8,128)}) %reduce-scatter.5.cloned.1.call-update) | async-done | bytes 65552 | tf_op jit(solution)/shard_map/reduce_scatter | solution.py:117
  395.7 78.8 %all-reduce.1 = (f32[16,16]{0,1:T(8,128)S(1)}, f32[16,16]{1,0:T(8,128)S(1)}) all-reduce(f32[16,16]{0,1:T(8,128)S(1)} %convolution_bitcast_fusion.1, f32[16,16]{1,0:T(8,128)S(1)} %fusion.72), channel_id=1, replica_groups=mesh['row'=16,'col'=16] {'row','col'}, use_global_device_ids=true, to_apply=%region_11.12 | all-reduce | flops 512 | bytes 4096 | tf_op jit(solution)/shard_map/psum | solution.py:122
  474.5 37.0 %while.135 = (s32[]{:T(128)}, f32[16,16]{1,0:T(8,128)S(1)}, f32[16,16]{1,0:T(8,128)S(1)}, s32[]{:T(128)}, s32[]{:T(128)}) while((s32[]{:T(128)}, f32[16,16]{1,0:T(8,128)S(1)}, f32[16,16]{1,0:T(8,128)S(1)}, s32[]{:T(128)}, s32[]{:T(128)}) %tuple.304), condition=%wide.region_10.11_spmd.clone.clone, body=%wide.region_4.10_spmd.clone.clone.sunk | while | flops 2978 | bytes 6069 | solution.py:28
  511.6 24.3 %while.129 = (s32[]{:T(128)}, f32[16,16]{1,0:T(8,128)S(1)}, f32[16,16]{1,0:T(8,128)S(1)}, f32[16,16]{1,0:T(8,128)S(1)}, s32[]{:T(128)}, /*index=5*/s32[]{:T(128)}) while((s32[]{:T(128)}, f32[16,16]{1,0:T(8,128)S(1)}, f32[16,16]{1,0:T(8,128)S(1)}, f32[16,16]{1,0:T(8,128)S(1)}, s32[]{:T(128)}, /*index=5*/s32[]{:T(128)}) %tuple.307), condition=%wide.region_17.18_spmd.clone, body=%wide.region_12.17_spmd.clone.sunk | while | flops 2626 | bytes 5984 | solution.py:43
  535.9 24.8 %while.130 = (s32[]{:T(128)}, f32[16,16]{1,0:T(8,128)S(1)}, f32[16,16]{1,0:T(8,128)S(1)}, f32[16,16]{1,0:T(8,128)S(1)}, s32[]{:T(128)}, /*index=5*/s32[]{:T(128)}, s32[]{:T(128)}) while((s32[]{:T(128)}, f32[16,16]{1,0:T(8,128)S(1)}, f32[16,16]{1,0:T(8,128)S(1)}, f32[16,16]{1,0:T(8,128)S(1)}, s32[]{:T(128)}, ...), condition=%wide.region_23.24_spmd.clone, body=%wide.region_18.23_spmd.clone.sunk | while | flops 2627 | bytes 6004 | solution.py:59
  561.0 19.6 %all_gather.11 = f32[16,8192]{1,0:T(8,128)S(1)} all-gather(f32[16,512]{1,0:T(8,128)S(1)} %convolution_subtract_fusion), channel_id=1, replica_groups=mesh['row'=16,'col'=16] {'row'}, dimensions={1}, use_global_device_ids=true | all-gather | bytes 557056 | tf_op jit(solution)/shard_map/all_gather | solution.py:134
  581.4 6.1 all-to-all-start
  587.7 3.8 convolution_multiply_fusion.1
  591.6 5.2 scatter_fusion.1
  597.7 7.6 all-to-all-done
  606.7 5.2 fusion.49
  613.4 175.2 %reduce-scatter.11.cloned.1.call-done = f32[16,512]{1,0:T(8,128)} async-done(((f32[16,8192]{1,0:T(8,128)}), f32[16,512]{1,0:T(8,128)}) %reduce-scatter.11.cloned.1.call-update) | async-done | bytes 32784 | tf_op jit(solution)/shard_map/reduce_scatter | solution.py:141
  788.6 65.7 %reduce-scatter.9.cloned.1.call-done = f32[16,512]{1,0:T(8,128)} async-done(((f32[16,8192]{1,0:T(8,128)}), f32[16,512]{1,0:T(8,128)}) %reduce-scatter.9.cloned.1.call-update) | async-done | bytes 32784 | tf_op jit(solution)/shard_map/reduce_scatter | solution.py:139
  854.3 0.9 fusion.58
  855.3 79.4 %all-reduce = (f32[48,48]{0,1:T(8,128)S(1)}, f32[48,48]{1,0:T(8,128)S(1)}) all-reduce(f32[48,48]{0,1:T(8,128)S(1)} %pad_maximum_fusion.1, f32[48,48]{1,0:T(8,128)S(1)} %fusion.70), channel_id=1, replica_groups=mesh['row'=16,'col'=16] {'row','col'}, use_global_device_ids=true, to_apply=%region_35.36 | all-reduce | flops 4608 | bytes 36864 | tf_op jit(solution)/shard_map/psum | solution.py:144
  934.9 111.3 %while.136 = (s32[]{:T(128)}, f32[48,48]{1,0:T(8,128)S(1)}, f32[48,48]{1,0:T(8,128)S(1)}, s32[]{:T(128)}, s32[]{:T(128)}) while((s32[]{:T(128)}, f32[48,48]{1,0:T(8,128)S(1)}, f32[48,48]{1,0:T(8,128)S(1)}, s32[]{:T(128)}, s32[]{:T(128)}) %tuple.313), condition=%wide.region_31.32_spmd.clone.clone, body=%wide.region_25.31_spmd.clone.clone.sunk | while | flops 25826 | bytes 48693 | solution.py:28
  1046.1 79.4 %while.131 = (s32[]{:T(128)}, f32[48,48]{1,0:T(8,128)S(1)}, f32[48,48]{1,0:T(8,128)S(1)}, f32[48,48]{1,0:T(8,128)S(1)}, s32[]{:T(128)}, /*index=5*/s32[]{:T(128)}) while((s32[]{:T(128)}, f32[48,48]{1,0:T(8,128)S(1)}, f32[48,48]{1,0:T(8,128)S(1)}, f32[48,48]{1,0:T(8,128)S(1)}, s32[]{:T(128)}, /*index=5*/s32[]{:T(128)}) %tuple.316), condition=%wide.region_41.42_spmd.clone, body=%wide.region_36.41_spmd.clone.sunk | while | flops 23234 | bytes 48480 | solution.py:43
  1125.6 79.4 %while.132 = (s32[]{:T(128)}, f32[48,48]{1,0:T(8,128)S(1)}, f32[48,48]{1,0:T(8,128)S(1)}, f32[48,48]{1,0:T(8,128)S(1)}, s32[]{:T(128)}, /*index=5*/s32[]{:T(128)}) while((s32[]{:T(128)}, f32[48,48]{1,0:T(8,128)S(1)}, f32[48,48]{1,0:T(8,128)S(1)}, f32[48,48]{1,0:T(8,128)S(1)}, s32[]{:T(128)}, /*index=5*/s32[]{:T(128)}) %tuple.346), condition=%wide.region_47.48_spmd.clone, body=%wide.region_42.47_spmd.clone.sunk | while | flops 23234 | bytes 48480 | solution.py:43
  1205.3 81.8 %while.133 = (s32[]{:T(128)}, f32[48,16]{0,1:T(8,128)S(1)}, f32[48,16]{0,1:T(8,128)S(1)}, f32[48,48]{1,0:T(8,128)S(1)}, s32[]{:T(128)}, /*index=5*/s32[]{:T(128)}, s32[]{:T(128)}) while((s32[]{:T(128)}, f32[48,16]{0,1:T(8,128)S(1)}, f32[48,16]{0,1:T(8,128)S(1)}, f32[48,48]{1,0:T(8,128)S(1)}, s32[]{:T(128)}, ...), condition=%wide.region_53.54_spmd.clone, body=%wide.region_48.53_spmd.clone.sunk | while | flops 10947 | bytes 23348 | solution.py:59
  1287.4 73.6 %psum.39 = f32[16,16]{1,0:T(8,128)S(1)} all-reduce(f32[16,16]{1,0:T(8,128)S(1)} %fusion.73), channel_id=1, replica_groups=mesh['row'=16,'col'=16] {'row','col'}, use_global_device_ids=true, to_apply=%region_54.55 | all-reduce | flops 256 | bytes 2048 | tf_op jit(solution)/shard_map/psum | solution.py:154
  1361.0 37.0 %while.137 = (s32[]{:T(128)}, f32[16,16]{1,0:T(8,128)S(1)}, f32[16,16]{1,0:T(8,128)S(1)}, s32[]{:T(128)}, s32[]{:T(128)}) while((s32[]{:T(128)}, f32[16,16]{1,0:T(8,128)S(1)}, f32[16,16]{1,0:T(8,128)S(1)}, s32[]{:T(128)}, s32[]{:T(128)}) %tuple.325), condition=%wide.region_61.62_spmd.clone.clone, body=%wide.region_55.61_spmd.clone.clone.sunk | while | flops 2978 | bytes 6069 | solution.py:28
  1398.0 26.3 %while.134 = (s32[]{:T(128)}, f32[16,512]{1,0:T(8,128)S(1)}, f32[16,512]{1,0:T(8,128)S(1)}, f32[16,16]{1,0:T(8,128)S(1)}, s32[]{:T(128)}, /*index=5*/s32[]{:T(128)}) while((s32[]{:T(128)}, f32[16,512]{1,0:T(8,128)S(1)}, f32[16,512]{1,0:T(8,128)S(1)}, f32[16,16]{1,0:T(8,128)S(1)}, s32[]{:T(128)}, /*index=5*/s32[]{:T(128)}) %tuple.328), condition=%wide.region_67.68_spmd.clone, body=%wide.region_62.67_spmd.clone.sunk | while | flops 66114 | bytes 144928 | solution.py:43
  (1702 shorter events, 407.7 us)
Async XLA Ops:
  7.2 41.9 %all-gather.5.cloned.1.call-start = ((), (), s32[]{:S(2)}) async-start(), calls=%async_computation.7 | async-start | bytes 1114112 | tf_op jit(solution)/shard_map/all_gather | solution.py:114
  8.7 0.6 copy-start.4
  9.4 117.1 %all-gather.3.cloned.1.call-start = ((), (), s32[]{:S(2)}) async-start(), calls=%async_computation.5 | async-start | bytes 1114112 | tf_op jit(solution)/shard_map/all_gather | solution.py:113
  10.1 318.2 %reduce-scatter.7.cloned.1.call-start = ((), (), s32[]{:S(2)}) async-start(), calls=%async_computation.8 | async-start | bytes 1114112 | tf_op jit(solution)/shard_map/reduce_scatter | solution.py:119
  61.7 333.0 %reduce-scatter.5.cloned.1.call-start = ((), (), s32[]{:S(2)}) async-start(), calls=%async_computation.6 | async-start | bytes 1114112 | tf_op jit(solution)/shard_map/reduce_scatter | solution.py:117
  134.6 1.2 copy-start.1
  561.0 726.1 %copy-start.2 = (f32[16,512]{1,0:T(8,128)}, f32[16,512]{1,0:T(8,128)S(1)}, u32[]{:S(2)}) copy-start(f32[16,512]{1,0:T(8,128)S(1)} %convolution_subtract_fusion) | copy-start | bytes 98308
  581.4 23.8 %all-to-all-start = ((f32[16,16,512]{2,1,0:T(8,128)}), f32[16,16,512]{2,1,0:T(8,128)S(1)}, u32[]{:S(2)}, u32[]{:S(2)}) async-start(f32[16,16,512]{2,1,0:T(8,128)} %stack.2), calls=%async_computation.2 | async-start | bytes 1048576 | tf_op jit(solution)/shard_map/all_to_all | solution.py:132
  587.5 201.1 %reduce-scatter.11.cloned.1.call-start = ((), (), s32[]{:S(2)}) async-start(), calls=%async_computation.10 | async-start | bytes 557056 | tf_op jit(solution)/shard_map/reduce_scatter | solution.py:141
  597.6 256.7 %reduce-scatter.9.cloned.1.call-start = ((), (), s32[]{:S(2)}) async-start(), calls=%async_computation.9 | async-start | bytes 557056 | tf_op jit(solution)/shard_map/reduce_scatter | solution.py:139
  606.7 6.1 copy-start.3
  1205.1 219.9 %copy-start = (f32[48,48]{1,0:T(8,128)}, f32[48,48]{1,0:T(8,128)S(1)}, u32[]{:S(2)}) copy-start(f32[48,48]{1,0:T(8,128)S(1)} %get-tuple-element.811) | copy-start | bytes 27652
Sparse Core Ops, SparseCore 0:
  9.8 39.1 all-gather.4
  51.6 74.7 all-gather.2
  130.3 198.0 reduce-scatter.6
  330.7 63.9 reduce-scatter.4
  597.7 190.8 reduce-scatter.10
  791.0 63.2 reduce-scatter.8
